TPU v7x, 512 devices: a whole 4x8x8 slice. The times are simulated.
512 devices in a mesh: ctx: 64 (over z, x, y_lo), tp: 8 (over y_hi, core).
Axes of the slice: x: 4, y: 8 (y_hi: 4, y_lo: 2; y = y_hi * 2 + y_lo), z: 8, core: 2. Of those that a mesh axis runs over, the one named last changes fastest.
Arguments:
- tokens: bfloat16 [8192, 4096], P('ctx'), may hold values from -6 to 6
- new_token_states: bfloat16 [4, 4096], replicated, may hold values from -6.0625 to 6.0625
- w_query: bfloat16 [4096, 2048], P('ctx', 'tp'), may hold values from -0.12162204 to 0.12162204
- key_matrix: bfloat16 [4096, 1024], P('ctx', 'tp'), may hold values from -0.12162204 to 0.12162204
- value_matrix: bfloat16 [4096, 1024], P('ctx', 'tp'), may hold values from -0.09375 to 0.09375
- w_out: bfloat16 [2048, 4096], P('tp', 'ctx'), may hold values from -0.125 to 0.125
- lengths: int32 [4], replicated, may hold values from 1 to 4096, 8192 in all
- block_map: int32 [128], replicated, may hold values from 0 to 127, each once
Outputs:
- prefill_out: bfloat16 [8192, 4096], P('ctx', 'tp')
- decode_out: bfloat16 [4, 4096], P(None, 'tp')
Inputs may be any that keep to these rules, and one draw needn't show every extreme that they name: The lengths sum to 8192, and some request has exactly 4096 tokens. `block_map`: each of the 128 initial blocks is held exactly once.
All inputs are finite; a program needn't handle non-finite values.
Results may differ from a plain program's by a relative error of at most 0.015.
Values may be sent and summed in bfloat16 or wider, within the bound.
A program may use at most 64 MiB of HBM per device.

v0:
```python
import math
import jax
import jax.numpy as jnp
from jax import lax
from jax.sharding import PartitionSpec as P

HEAD_SIZE = 128
floor_value = -1e30


def initial_positions(block_map, first_row, row_count, block_rows):
    row_ids = first_row + jnp.arange(row_count, dtype=jnp.int32)
    block_ids = row_ids // block_rows
    table_ids = jnp.arange(block_map.shape[0], dtype=jnp.int32)
    mapped = jnp.sum(
        jnp.where(block_ids[:, None] == table_ids[None, :], block_map[None, :], 0), axis=1
    )
    return mapped * block_rows + row_ids % block_rows


def request_index(positions, request_ends):
    return jnp.sum((positions[:, None] >= request_ends[None, :]).astype(jnp.int32), axis=1)


def round_weights(weights):
    rounded = weights.astype(jnp.bfloat16)
    rounded = lax.optimization_barrier(rounded)
    return rounded.astype(jnp.float32)


def softmax_parts(
    dec_heads, projected_key_rows, projected_value_rows, owned, kv_heads, head_dim, score_scale
):
    row_count = projected_key_rows.shape[0]
    scores = (
        jnp.einsum(
            "rgjd,tgd->rgjt",
            dec_heads,
            projected_key_rows.reshape(row_count, kv_heads, head_dim),
            preferred_element_type=jnp.float32,
        )
        * score_scale
    )
    scores = jnp.where(owned, scores, floor_value)
    part_peak = jnp.max(scores, axis=3)
    weights = jnp.where(owned, jnp.exp(scores - part_peak[..., None]), 0.0)
    part_total = jnp.sum(weights, axis=3)
    part_mixed = jnp.einsum(
        "rgjt,tgd->rgjd",
        weights.astype(jnp.bfloat16),
        projected_value_rows.reshape(row_count, kv_heads, head_dim),
        preferred_element_type=jnp.float32,
    )
    return (part_peak, part_total, part_mixed)


def on_device(
    tokens, new_token_states, w_query, key_matrix, value_matrix, w_out, lengths, block_map
):
    local_rows = tokens.shape[0]
    block_rows = local_rows // 2
    request_count = new_token_states.shape[0]
    head_dim = HEAD_SIZE
    query_width = w_query.shape[1]
    kv_width = key_matrix.shape[1]
    kv_heads = kv_width // head_dim
    query_group_count = query_width // kv_width
    score_scale = 1.0 / math.sqrt(head_dim)
    device = lax.axis_index("ctx")
    request_ends = jnp.cumsum(lengths)
    inputs = jnp.concatenate([tokens, new_token_states], axis=0)
    shard_pieces = (
        lax.all_gather(w_query, "ctx", axis=0, tiled=True),
        lax.all_gather(key_matrix, "ctx", axis=0, tiled=True),
        lax.all_gather(value_matrix, "ctx", axis=0, tiled=True),
    )
    query_all, key_all, value_all = tuple(
        (jnp.dot(inputs, weight, preferred_element_type=jnp.float32) for weight in shard_pieces)
    )
    query_all = query_all.astype(jnp.bfloat16)
    key_all = key_all.astype(jnp.bfloat16)
    value_all = value_all.astype(jnp.bfloat16)
    local_query = query_all[:local_rows]
    local_keys = key_all[:local_rows]
    local_values = value_all[:local_rows]
    dec_query = query_all[local_rows:]
    decode_key_rows = key_all[local_rows:]
    decode_value_rows = value_all[local_rows:]
    token_pos = initial_positions(block_map, device * local_rows, local_rows, block_rows)
    token_request = request_index(token_pos, request_ends)
    query_heads = local_query.reshape(local_rows, kv_heads, query_group_count, head_dim)

    def attend(running, shard_pieces, first_row):
        peak_run, total_run, mixed_run = running
        key_piece, value_piece = shard_pieces
        row_count = key_piece.shape[0]
        key_pos = initial_positions(block_map, first_row, row_count, block_rows)
        key_request = request_index(key_pos, request_ends)
        allowed = (key_request[None, :] == token_request[:, None]) & (
            key_pos[None, :] <= token_pos[:, None]
        )
        scores = (
            jnp.einsum(
                "tgjd,kgd->gjtk",
                query_heads,
                key_piece.reshape(row_count, kv_heads, head_dim),
                preferred_element_type=jnp.float32,
            )
            * score_scale
        )
        scores = jnp.where(allowed, scores, floor_value)
        peak_new = jnp.maximum(peak_run, jnp.max(scores, axis=3))
        weights = jnp.where(allowed, jnp.exp(scores - peak_new[..., None]), 0.0)
        rescale = jnp.exp(peak_run - peak_new)
        total_new = total_run * rescale + jnp.sum(weights, axis=3)
        mixed_new = mixed_run * rescale[..., None] + jnp.einsum(
            "gjtk,kgd->gjtd",
            weights.astype(jnp.bfloat16),
            value_piece.reshape(row_count, kv_heads, head_dim),
            preferred_element_type=jnp.float32,
        )
        return (peak_new, total_new, mixed_new)

    start_state = (
        jnp.full((kv_heads, query_group_count, local_rows), floor_value, jnp.float32),
        jnp.zeros((kv_heads, query_group_count, local_rows), jnp.float32),
        jnp.zeros((kv_heads, query_group_count, local_rows, head_dim), jnp.float32),
    )
    dec_heads = dec_query.reshape(request_count, kv_heads, query_group_count, head_dim)
    request_ids = jnp.arange(request_count, dtype=jnp.int32)
    cache_keys, cache_values = (
        lax.all_gather(local_keys, "ctx", axis=0, tiled=True),
        lax.all_gather(local_values, "ctx", axis=0, tiled=True),
    )
    total_rows = cache_keys.shape[0]
    shard_count = total_rows // local_rows
    limit = max(1, 1024 // local_rows)
    step_rows = local_rows * math.gcd(shard_count, 1 << limit.bit_length() - 1)

    def key_step(running, step_index):
        first_row = step_index * step_rows
        pieces = (
            lax.dynamic_slice_in_dim(cache_keys, first_row, step_rows, 0),
            lax.dynamic_slice_in_dim(cache_values, first_row, step_rows, 0),
        )
        return (attend(running, pieces, first_row), None)

    final_state, unused = lax.scan(
        key_step, start_state, jnp.arange(total_rows // step_rows, dtype=jnp.int32)
    )
    peak_run, total_run, mixed_run = final_state
    cache_pos = (
        block_map[:, None] * block_rows + jnp.arange(block_rows, dtype=jnp.int32)[None, :]
    ).reshape(total_rows)
    cache_request = request_index(cache_pos, request_ends)
    owned = (cache_request[None, :] == request_ids[:, None])[:, None, None, :]
    cache_peak, cache_total, cache_mixed = softmax_parts(
        dec_heads, cache_keys, cache_values, owned, kv_heads, head_dim, score_scale
    )
    attended = (
        (mixed_run / total_run[..., None]).transpose(2, 0, 1, 3).reshape(local_rows, query_width)
    )
    attended = attended.astype(jnp.bfloat16)
    own_keys = decode_key_rows.reshape(request_count, kv_heads, 1, head_dim).astype(jnp.float32)
    own_values = decode_value_rows.reshape(request_count, kv_heads, 1, head_dim).astype(jnp.float32)
    self_scores = jnp.sum(dec_heads.astype(jnp.float32) * own_keys, axis=3) * score_scale
    peak_all = jnp.maximum(cache_peak, self_scores)
    rescale = jnp.exp(cache_peak - peak_all)
    self_weights = jnp.exp(self_scores - peak_all)
    dec_total = cache_total * rescale + self_weights
    dec_mixed = (
        cache_mixed * rescale[..., None] + round_weights(self_weights)[..., None] * own_values
    )
    dec_attn = (
        (dec_mixed / dec_total[..., None]).reshape(request_count, query_width).astype(jnp.bfloat16)
    )
    attended_all = jnp.concatenate([attended, dec_attn], axis=0)
    projected = jnp.dot(
        attended_all,
        lax.all_gather(w_out, "ctx", axis=1, tiled=True),
        preferred_element_type=jnp.float32,
    )
    summed_rows = lax.psum_scatter(
        projected.astype(jnp.bfloat16), "tp", scatter_dimension=1, tiled=True
    ).astype(jnp.float32)
    summed_rows = summed_rows.astype(jnp.bfloat16)
    return (summed_rows[:local_rows], summed_rows[local_rows:])


def solution(mesh):
    return jax.shard_map(
        on_device,
        mesh=mesh,
        in_specs=(
            P("ctx", None),
            P(),
            P("ctx", "tp"),
            P("ctx", "tp"),
            P("ctx", "tp"),
            P("tp", "ctx"),
            P(),
            P(),
        ),
        out_specs=(P("ctx", "tp"), P(None, "tp")),
        check_vma=False,
    )
```

profile of v0, /device:TPU:17, one launch (start us, length us, event | category | flops | bytes accessed | tf_op | source)
XLA Modules:
  0.0 1876.2 jit_solution(13340912142481138147)
XLA Ops:
  7.2 0.7 all-gather.7.cloned.1.call-update
  8.0 0.7 all-gather.13.cloned.1.call-update
  8.7 0.7 all-gather.11.cloned.1.call-update
  9.4 1.3 constant_dynamic-update-slice_fusion.1
  10.8 258.8 %all-gather.7.cloned.1.call-done = bf16[4096,128]{1,0:T(8,128)(2,1)} async-done(((bf16[64,128]{1,0:T(8,128)(2,1)}), bf16[4096,128]{1,0:T(8,128)(2,1)}) %all-gather.7.cloned.1.call-update) | async-done | bytes 1048592 | tf_op jit(solution)/shard_map/all_gather | solution.py:74
  269.6 1.7 convolution_convert_fusion.3
  271.2 0.6 slice.32
  271.9 296.3 %all-gather.13.cloned.1.call-done = bf16[4096,128]{1,0:T(8,128)(2,1)} async-done(((bf16[64,128]{1,0:T(8,128)(2,1)}), bf16[4096,128]{1,0:T(8,128)(2,1)}) %all-gather.13.cloned.1.call-update) | async-done | bytes 1048592 | tf_op jit(solution)/shard_map/all_gather | solution.py:75
  568.3 1.7 convolution_convert_fusion.2
  570.0 0.6 slice.34
  570.6 0.5 all-gather.17.cloned.1.call-update
  572.1 300.8 %all-gather.11.cloned.1.call-done = bf16[4096,256]{1,0:T(8,128)(2,1)} async-done(((bf16[64,256]{1,0:T(8,128)(2,1)}), bf16[4096,256]{1,0:T(8,128)(2,1)}) %all-gather.11.cloned.1.call-update) | async-done | bytes 2097168 | tf_op jit(solution)/shard_map/all_gather | solution.py:73
  872.9 2.1 convolution_convert_fusion.1
  875.2 300.6 %all-gather.9.cloned.1.call-done = bf16[8192,128]{1,0:T(8,128)(2,1)} async-done(((bf16[128,128]{1,0:T(8,128)(2,1)}), bf16[8192,128]{1,0:T(8,128)(2,1)}) %all-gather.9.cloned.1.call-update) | async-done | bytes 2097168 | tf_op jit(solution)/shard_map/all_gather | solution.py:132
  1175.8 302.3 %all-gather.15.cloned.1.call-done = bf16[8192,128]{1,0:T(8,128)(2,1)} async-done(((bf16[128,128]{1,0:T(8,128)(2,1)}), bf16[8192,128]{1,0:T(8,128)(2,1)}) %all-gather.15.cloned.1.call-update) | async-done | bytes 2097168 | tf_op jit(solution)/shard_map/all_gather | solution.py:133
  1478.1 40.4 %while.17 = (s32[]{:T(128)}, f32[1,2,128]{2,1,0:T(2,128)S(1)}, f32[1,2,128]{2,1,0:T(2,128)S(1)}, f32[1,2,128,128]{3,2,1,0:T(8,128)S(1)}, s32[8]{0:T(128)S(1)}, /...) while((s32[]{:T(128)}, f32[1,2,128]{2,1,0:T(2,128)S(1)}, ...), condition=%wide.region_8.9_spmd.clone, body=%wide.region_3.8_spmd.clone.sunk | while | flops 137504256 | bytes 4577019 | solution.py:148
  1478.1 0.6 dynamic_slice.37
  1479.3 0.4 select_reduce_fusion.3
  1480.2 1.3 fusion.90
  1481.5 1.4 fusion.93
  1483.1 0.6 dynamic_slice.37
  1485.2 1.3 fusion.90
  1486.5 1.4 fusion.93
  1488.2 0.6 dynamic_slice.37
  1490.3 1.3 fusion.90
  1491.6 1.4 fusion.93
  1493.2 0.6 dynamic_slice.37
  1495.3 1.3 fusion.90
  1496.6 1.4 fusion.93
  1498.3 0.6 dynamic_slice.37
  1500.4 1.3 fusion.90
  1501.7 1.4 fusion.93
  1503.3 0.6 dynamic_slice.37
  1505.4 1.3 fusion.90
  1506.7 1.4 fusion.93
  1508.4 0.6 dynamic_slice.37
  1510.5 1.3 fusion.90
  1511.8 1.4 fusion.93
  1513.4 0.6 dynamic_slice.37
  1515.5 1.3 fusion.90
  1516.8 1.4 fusion.93
  1518.5 2.5 fusion.72
  1521.3 0.5 fusion.48
  1522.1 258.3 %all-gather.17.cloned.1.call-done = bf16[256,4096]{0,1:T(8,128)(2,1)} async-done(((bf16[256,64]{0,1:T(8,128)(2,1)}), bf16[256,4096]{0,1:T(8,128)(2,1)}) %all-gather.17.cloned.1.call-update) | async-done | bytes 2097168 | tf_op jit(solution)/shard_map/all_gather | solution.py:180
  1780.4 3.4 convolution_convert_fusion
  1783.8 82.6 %reduce-scatter.2.cloned.1.call-done = bf16[132,512]{1,0:T(8,128)(2,1)} async-done(((bf16[132,4096]{1,0:T(8,128)(2,1)}), bf16[132,512]{1,0:T(8,128)(2,1)}) %reduce-scatter.2.cloned.1.call-update) | async-done | bytes 135184 | tf_op jit(solution)/shard_map/reduce_scatter | solution.py:183
  1866.5 1.6 slice.38
  1868.0 1.3 slice.39
  (120 shorter events, 10.1 us)
Async XLA Ops:
  7.2 3.6 copy-start
  7.2 262.4 %all-gather.7.cloned.1.call-start = ((), (), s32[]{:S(2)}) async-start(), calls=%async_computation.1 | async-start | bytes 1064960 | tf_op jit(solution)/shard_map/all_gather | solution.py:74
  7.9 560.4 %all-gather.13.cloned.1.call-start = ((), (), s32[]{:S(2)}) async-start(), calls=%async_computation.4 | async-start | bytes 1064960 | tf_op jit(solution)/shard_map/all_gather | solution.py:75
  8.7 864.2 %all-gather.11.cloned.1.call-start = ((), (), s32[]{:S(2)}) async-start(), calls=%async_computation.3 | async-start | bytes 2129920 | tf_op jit(solution)/shard_map/all_gather | solution.py:73
  9.4 1166.4 %all-gather.9.cloned.1.call-start = ((), (), s32[]{:S(2)}) async-start(), calls=%async_computation.2 | async-start | bytes 2129920 | tf_op jit(solution)/shard_map/all_gather | solution.py:132
  10.8 560.5 %copy-start.3 = (s32[4]{0:T(128)S(1)}, s32[4]{0:T(128)}, u32[]{:S(2)}) copy-start(s32[4]{0:T(128)} %param.16) | copy-start | bytes 52
  10.8 560.6 %copy-start.1 = (s32[128]{0:T(128)S(1)}, s32[128]{0:T(128)}, u32[]{:S(2)}) copy-start(s32[128]{0:T(128)} %param.17) | copy-start | bytes 1540
  271.9 1206.2 %all-gather.15.cloned.1.call-start = ((), (), s32[]{:S(2)}) async-start(), calls=%async_computation.5 | async-start | bytes 2129920 | tf_op jit(solution)/shard_map/all_gather | solution.py:133
  570.6 1209.8 %all-gather.17.cloned.1.call-start = ((), (), s32[]{:S(2)}) async-start(), calls=%async_computation.6 | async-start | bytes 2129920 | tf_op jit(solution)/shard_map/all_gather | solution.py:180
  571.2 1295.3 %reduce-scatter.2.cloned.1.call-start = ((), (), s32[]{:S(2)}) async-start(), calls=%async_computation.7 | async-start | bytes 1253376 | tf_op jit(solution)/shard_map/reduce_scatter | solution.py:183
  1518.5 2.8 copy-start.2
Sparse Core Ops, SparseCore 0:
  10.1 259.4 all-gather.6
  271.6 296.5 all-gather.12
  570.4 302.4 all-gather.10
  875.4 300.3 all-gather.8
  1177.7 300.3 all-gather.14
  1480.0 300.3 all-gather.16
  1783.9 82.4 reduce-scatter.1
where the time goes:
time: 1880 us
  waiting for transfers between devices  1800 us (96%)
  matrix products  33.2 us (2%)
    all_gather x1, waiting for transfers between devices, on_device(): lax.all_gather(local_values, 'ctx', axis=0, tiled=True)  302 us
    all_gather x1, waiting for transfers between devices, on_device(): lax.all_gather(w_query, 'ctx', axis=0, tiled=True)  301 us
    all_gather x1, waiting for transfers between devices, on_device(): lax.all_gather(local_keys, 'ctx', axis=0, tiled=True)  301 us
    all_gather x1, waiting for transfers between devices, on_device(): lax.all_gather(value_matrix, 'ctx', axis=0, tiled=True)  296 us
    all_gather x1, waiting for transfers between devices, on_device(): lax.all_gather(key_matrix, 'ctx', axis=0, tiled=True)  259 us
    all_gather x1, waiting for transfers between devices, on_device(): lax.all_gather(w_out, 'ctx', axis=1, tiled=True)  258 us
    reduce_scatter x1, waiting for transfers between devices, on_device(): lax.psum_scatter(projected.astype(jnp.bfloat16), 'tp', scatter_dimension=...  82.6 us
  transfers between devices with their start and end apart: 7, of which 7 were waited for; matrix products, arithmetic and copies ran while one was open for 3% of the time, Pallas kernels for 0%

commit v1 on v0

--- a/solution.py
+++ b/solution.py
@@ -71,7 +71,9 @@
     inputs = jnp.concatenate([tokens, new_token_states], axis=0)
     shard_pieces = (
         lax.all_gather(w_query, "ctx", axis=0, tiled=True),
-        lax.all_gather(key_matrix, "ctx", axis=0, tiled=True),
+        jnp.concatenate(
+            lax.all_to_all(jnp.stack([key_matrix] * lax.axis_size("ctx")), "ctx", 0, 0), axis=0
+        ),
         lax.all_gather(value_matrix, "ctx", axis=0, tiled=True),
     )
     query_all, key_all, value_all = tuple(

time: 1880 us -> 1580 us (0.84)
  waiting for transfers between devices: 1800 us -> 1490 us
    all_gather x1 -> x0, waiting for transfers between devices: 259 us -> none  [on_device(): lax.all_gather(key_matrix, 'ctx', axis=0, tiled=True)]
    all_gather x1, waiting for transfers between devices: 296 us -> 218 us  [on_device(): lax.all_gather(value_matrix, 'ctx', axis=0, tiled=True)]
    all_to_all x0 -> x1, waiting for transfers between devices: none -> 26.4 us  [on_device(): lax.all_to_all(jnp.stack([key_matrix] * lax.axis_size('ctx')), 'ctx', 0, 0)]
where the time goes in v1:
time: 1580 us
  waiting for transfers between devices  1490 us (94%)
  matrix products  32.1 us (2%)
    all_gather x1, waiting for transfers between devices, on_device(): lax.all_gather(local_values, 'ctx', axis=0, tiled=True)  302 us
    all_gather x1, waiting for transfers between devices, on_device(): lax.all_gather(local_keys, 'ctx', axis=0, tiled=True)  301 us
    all_gather x1, waiting for transfers between devices, on_device(): lax.all_gather(w_query, 'ctx', axis=0, tiled=True)  300 us
    all_gather x1, waiting for transfers between devices, on_device(): lax.all_gather(w_out, 'ctx', axis=1, tiled=True)  258 us
    all_gather x1, waiting for transfers between devices, on_device(): lax.all_gather(value_matrix, 'ctx', axis=0, tiled=True)  218 us
    reduce_scatter x1, waiting for transfers between devices, on_device(): lax.psum_scatter(projected.astype(jnp.bfloat16), 'tp', scatter_dimension=...  82.5 us
  transfers between devices with their start and end apart: 7, of which 7 were waited for; matrix products, arithmetic and copies ran while one was open for 3% of the time, Pallas kernels for 0%

profile of v1, /device:TPU:17, one launch (start us, length us, event | category | flops | bytes accessed | tf_op | source)
XLA Modules:
  0.0 1578.3 jit_solution(1833813509447543973)
XLA Ops:
  7.2 0.7 all-gather.10.cloned.1.call-update
  8.0 0.7 all-gather.8.cloned.1.call-update
  8.7 2.0 stack.2
  10.6 14.6 all-to-all-start
  25.5 26.4 %all-to-all-done = bf16[64,64,128]{2,1,0:T(8,128)(2,1)S(1)} async-done(((bf16[64,64,128]{2,1,0:T(8,128)(2,1)}), bf16[64,64,128]{2,1,0:T(8,128)(2,1)S(1)}, u32[]{:S(2)}, u32[]{:S(2)}) %all-to-all-start) | async-done | bytes 1048608 | tf_op jit(solution)/shard_map/all_to_all | solution.py:75
  51.9 0.5 convolution_convert_fusion.3
  52.3 0.6 slice.32
  53.0 218.1 %all-gather.10.cloned.1.call-done = bf16[4096,128]{1,0:T(8,128)(2,1)} async-done(((bf16[64,128]{1,0:T(8,128)(2,1)}), bf16[4096,128]{1,0:T(8,128)(2,1)}) %all-gather.10.cloned.1.call-update) | async-done | bytes 1048592 | tf_op jit(solution)/shard_map/all_gather | solution.py:77
  271.1 1.7 convolution_convert_fusion.2
  272.8 0.6 slice.34
  273.5 0.5 all-gather.14.cloned.1.call-update
  275.0 299.8 %all-gather.8.cloned.1.call-done = bf16[4096,256]{1,0:T(8,128)(2,1)} async-done(((bf16[64,256]{1,0:T(8,128)(2,1)}), bf16[4096,256]{1,0:T(8,128)(2,1)}) %all-gather.8.cloned.1.call-update) | async-done | bytes 2097168 | tf_op jit(solution)/shard_map/all_gather | solution.py:73
  574.8 2.1 convolution_convert_fusion.1
  577.2 300.7 %all-gather.6.cloned.1.call-done = bf16[8192,128]{1,0:T(8,128)(2,1)} async-done(((bf16[128,128]{1,0:T(8,128)(2,1)}), bf16[8192,128]{1,0:T(8,128)(2,1)}) %all-gather.6.cloned.1.call-update) | async-done | bytes 2097168 | tf_op jit(solution)/shard_map/all_gather | solution.py:134
  877.9 302.3 %all-gather.12.cloned.1.call-done = bf16[8192,128]{1,0:T(8,128)(2,1)} async-done(((bf16[128,128]{1,0:T(8,128)(2,1)}), bf16[8192,128]{1,0:T(8,128)(2,1)}) %all-gather.12.cloned.1.call-update) | async-done | bytes 2097168 | tf_op jit(solution)/shard_map/all_gather | solution.py:135
  1180.2 40.4 %while.17 = (s32[]{:T(128)}, f32[1,2,128]{2,1,0:T(2,128)S(1)}, f32[1,2,128]{2,1,0:T(2,128)S(1)}, f32[1,2,128,128]{3,2,1,0:T(8,128)S(1)}, s32[8]{0:T(128)S(1)}, /...) while((s32[]{:T(128)}, f32[1,2,128]{2,1,0:T(2,128)S(1)}, ...), condition=%wide.region_8.9_spmd.clone, body=%wide.region_3.8_spmd.clone.sunk | while | flops 137504256 | bytes 4577019 | solution.py:150
  1180.2 0.6 dynamic_slice.37
  1182.3 1.3 fusion.90
  1183.6 1.4 fusion.93
  1185.2 0.6 dynamic_slice.37
  1187.3 1.3 fusion.90
  1188.6 1.4 fusion.93
  1190.3 0.6 dynamic_slice.37
  1191.5 0.4 select_reduce_fusion.3
  1192.4 1.3 fusion.90
  1193.7 1.4 fusion.93
  1195.3 0.6 dynamic_slice.37
  1197.4 1.3 fusion.90
  1198.7 1.4 fusion.93
  1200.4 0.6 dynamic_slice.37
  1202.5 1.3 fusion.90
  1203.8 1.4 fusion.93
  1205.4 0.6 dynamic_slice.37
  1207.5 1.3 fusion.90
  1208.8 1.4 fusion.93
  1210.5 0.6 dynamic_slice.37
  1212.6 1.3 fusion.90
  1213.9 1.4 fusion.93
  1215.6 0.6 dynamic_slice.37
  1217.6 1.3 fusion.90
  1219.0 1.4 fusion.93
  1220.6 2.5 fusion.72
  1223.4 0.5 fusion.48
  1224.2 258.4 %all-gather.14.cloned.1.call-done = bf16[256,4096]{0,1:T(8,128)(2,1)} async-done(((bf16[256,64]{0,1:T(8,128)(2,1)}), bf16[256,4096]{0,1:T(8,128)(2,1)}) %all-gather.14.cloned.1.call-update) | async-done | bytes 2097168 | tf_op jit(solution)/shard_map/all_gather | solution.py:182
  1482.6 3.4 convolution_convert_fusion
  1486.1 82.5 %reduce-scatter.2.cloned.1.call-done = bf16[132,512]{1,0:T(8,128)(2,1)} async-done(((bf16[132,4096]{1,0:T(8,128)(2,1)}), bf16[132,512]{1,0:T(8,128)(2,1)}) %reduce-scatter.2.cloned.1.call-update) | async-done | bytes 135184 | tf_op jit(solution)/shard_map/reduce_scatter | solution.py:185
  1568.6 1.6 slice.38
  1570.2 1.3 slice.39
  (122 shorter events, 10.2 us)
Async XLA Ops:
  7.2 18.2 %copy-start = (bf16[128,4096]{1,0:T(8,128)(2,1)S(1)}, bf16[128,4096]{1,0:T(8,128)(2,1)}, u32[]{:S(2)}) copy-start(bf16[128,4096]{1,0:T(8,128)(2,1)} %param.10) | copy-start | bytes 3145732
  7.2 263.9 %all-gather.10.cloned.1.call-start = ((), (), s32[]{:S(2)}) async-start(), calls=%async_computation.4 | async-start | bytes 1064960 | tf_op jit(solution)/shard_map/all_gather | solution.py:77
  7.9 566.9 %all-gather.8.cloned.1.call-start = ((), (), s32[]{:S(2)}) async-start(), calls=%async_computation.3 | async-start | bytes 2129920 | tf_op jit(solution)/shard_map/all_gather | solution.py:73
  10.6 14.8 copy-start.1
  10.6 41.3 %all-to-all-start = ((bf16[64,64,128]{2,1,0:T(8,128)(2,1)}), bf16[64,64,128]{2,1,0:T(8,128)(2,1)S(1)}, u32[]{:S(2)}, u32[]{:S(2)}) async-start(bf16[64,64,128]{2,1,0:T(8,128)(2,1)} %stack.2), calls=%async_computation | async-start | bytes 2097152 | tf_op jit(solution)/shard_map/all_to_all | solution.py:75
  25.3 852.6 %all-gather.6.cloned.1.call-start = ((), (), s32[]{:S(2)}) async-start(), calls=%async_computation.2 | async-start | bytes 2129920 | tf_op jit(solution)/shard_map/all_gather | solution.py:134
  51.9 222.3 %copy-start.4 = (s32[4]{0:T(128)S(1)}, s32[4]{0:T(128)}, u32[]{:S(2)}) copy-start(s32[4]{0:T(128)} %param.16) | copy-start | bytes 52
  51.9 222.4 %copy-start.2 = (s32[128]{0:T(128)S(1)}, s32[128]{0:T(128)}, u32[]{:S(2)}) copy-start(s32[128]{0:T(128)} %param.17) | copy-start | bytes 1540
  53.0 1127.2 %all-gather.12.cloned.1.call-start = ((), (), s32[]{:S(2)}) async-start(), calls=%async_computation.5 | async-start | bytes 2129920 | tf_op jit(solution)/shard_map/all_gather | solution.py:135
  273.5 1209.2 %all-gather.14.cloned.1.call-start = ((), (), s32[]{:S(2)}) async-start(), calls=%async_computation.6 | async-start | bytes 2129920 | tf_op jit(solution)/shard_map/all_gather | solution.py:182
  274.0 1294.5 %reduce-scatter.2.cloned.1.call-start = ((), (), s32[]{:S(2)}) async-start(), calls=%async_computation.7 | async-start | bytes 1253376 | tf_op jit(solution)/shard_map/reduce_scatter | solution.py:185
  1220.6 2.8 copy-start.3
Sparse Core Ops, SparseCore 0:
  10.1 260.9 all-gather.9
  273.2 301.5 all-gather.7
  577.5 300.3 all-gather.5
  879.8 300.3 all-gather.11
  1182.1 300.4 all-gather.13
  1486.2 82.3 reduce-scatter.1
